TPU v7x, 512 devices: a whole 4x4x16 slice. The times are simulated.
512 devices in a mesh: ctx: 32 (over y_lo, z), fsdp: 16 (over y_hi, x, core).
Axes of the slice: x: 4, y: 4 (y_hi: 2, y_lo: 2; y = y_hi * 2 + y_lo), z: 16, core: 2. Of those that a mesh axis runs over, the one named last changes fastest.
Arguments:
- sig_raw: bfloat16 [4096, 8192], P('ctx', 'fsdp'), may hold values from -6 to 6
- map_raw: bfloat16 [4096, 2048], P('ctx'), may hold values from -1.796875 to 1.796875
- step_size_logits: float32 [4096, 128], P('ctx', 'fsdp'), may hold values from -5.4 to 21.5
- d_out: bfloat16 [4096, 8192], P('ctx', 'fsdp'), may hold values from -6 to 6
- sig_taps: float32 [4, 8192], P(None, 'fsdp'), may hold values from -3 to 3
- map_taps: float32 [4, 2048], P(None, 'fsdp'), may hold values from -3 to 3
- sig_bias: float32 [8192], P('fsdp'), may hold values from -3 to 3
- map_bias: float32 [2048], P('fsdp'), may hold values from -0.6 to 0.6
- a_log: float32 [128], P('fsdp'), as said below
- dt_bias: float32 [128], P('fsdp'), may hold values from -5 to -4.2
- skip_gain: float32 [128], P('fsdp'), may hold values from 0.1 to 3
Outputs:
- d_sig: float32 [4096, 8192], P('ctx', 'fsdp')
- d_map: float32 [4096, 2048], P('ctx', 'fsdp')
- d_dt: float32 [4096, 128], P('ctx', 'fsdp')
- d_sig_taps: float32 [4, 8192], P(None, 'fsdp')
- d_map_taps: float32 [4, 2048], P(None, 'fsdp')
- d_sig_bias: float32 [8192], P('fsdp')
- d_map_bias: float32 [2048], P('fsdp')
- d_a_log: float32 [128], P('fsdp')
- scaled_timestep_shift_grad: float32 [128], P('fsdp')
- d_skip: float32 [128], P('fsdp')
Inputs may be any that keep to these rules, and one draw needn't show every extreme that they name: Each head's rate exp(a_log) lies either between 2 and 4 or between 30 / 4096 and 200 / 4096.
All inputs are finite; a program needn't handle non-finite values.
Results may differ from a plain program's by a relative error of at most 0.0066.
Values may be sent and summed in bfloat16 or wider, within the bound.
A program may use at most 128 MiB of HBM per device.

v0:
```python
import math
import jax
import jax.numpy as jnp
from jax import lax
from jax.sharding import PartitionSpec as P

HEADS = 128
HDIM = 64
STATE = 128
GROUPS = 8


def prefix(part, axis, combine, identity, reverse):
    count = lax.axis_size(axis)
    place = lax.axis_index(axis)
    ahead = count - 1 - place if reverse else place
    gathered = jax.tree.map(lambda a: lax.all_gather(a, axis), part)
    state = jax.tree.map(lambda a, e: jnp.zeros_like(a) + jnp.asarray(e, a.dtype), part, identity)

    def one(lap, state):
        source = count - 1 - lap if reverse else lap
        return combine(
            state, jax.tree.map(lambda a: lax.dynamic_index_in_dim(a, source, 0, False), gathered)
        )

    return lax.fori_loop(0, ahead, one, state)


def broadcast(x, axis, root):
    mine = lax.axis_index(axis) == root
    return lax.psum(jnp.where(mine, x, jnp.zeros_like(x)), axis)


def extended(block, sides, width):
    for axis, dim in sides:
        count = lax.axis_size(axis)
        forward = [(i, i + 1) for i in range(count - 1)]
        backward = [(target, source) for source, target in forward]
        low = lax.ppermute(
            lax.slice_in_dim(block, block.shape[dim] - width, None, axis=dim), axis, forward
        )
        high = lax.ppermute(lax.slice_in_dim(block, 0, width, axis=dim), axis, backward)
        block = jnp.concatenate([low, block, high], axis=dim)
    return block


def ein(form, left, right):
    return jnp.einsum(form, left, right, preferred_element_type=jnp.float32)


def silu_slope(value):
    sig = jax.nn.sigmoid(value)
    return sig * (1.0 + value * (1.0 - sig))


def block_parts(activated, dt_rows, a_log, dt_bias, groups):
    length = activated.shape[0]
    heads = dt_rows.shape[1]
    inner = heads * HDIM
    shared = groups * STATE
    ratio = heads // groups
    signal = activated[:, :inner].reshape(length, heads, HDIM)
    input_map = activated[:, inner : inner + shared].reshape(length, groups, STATE)
    output_map = activated[:, inner + shared :].reshape(length, groups, STATE)
    input_heads = jnp.repeat(input_map, ratio, axis=1)
    output_heads = jnp.repeat(output_map, ratio, axis=1)
    step = jax.nn.softplus(dt_rows + dt_bias)
    rate = -jnp.exp(a_log)
    row_ids = lax.broadcasted_iota(jnp.int32, (length, length), 0)
    col_ids = lax.broadcasted_iota(jnp.int32, (length, length), 1)
    lower = (row_ids >= col_ids).astype(jnp.float32)
    decay_sum = jnp.dot(lower, step * rate, precision=lax.Precision.HIGHEST)
    to_end = jnp.exp(decay_sum[-1][None, :] - decay_sum)
    scaled = (signal.astype(jnp.float32) * step[:, :, None]).astype(jnp.bfloat16)
    weighted = (scaled.astype(jnp.float32) * to_end[:, :, None]).astype(jnp.bfloat16)
    local = ein("qhp,qhn->hpn", weighted, input_heads)
    return (
        signal,
        input_map,
        output_map,
        input_heads,
        output_heads,
        step,
        rate,
        lower,
        decay_sum,
        scaled,
        to_end,
        weighted,
        local,
    )


def entry_grad(parts, d_rows):
    decay_sum = parts[8]
    output_heads = parts[4]
    scaled_grad = (d_rows.astype(jnp.float32) * jnp.exp(decay_sum)[:, :, None]).astype(jnp.bfloat16)
    return (scaled_grad, ein("thp,thn->hpn", scaled_grad, output_heads))


def block_grads(parts, d_rows, scaled_grad, h_in, carried, skip_gain, dt_rows, dt_bias):
    (
        signal,
        input_map,
        output_map,
        input_heads,
        output_heads,
        step,
        rate,
        lower,
        decay_sum,
        scaled,
        to_end,
        weighted,
        local,
    ) = parts
    length = d_rows.shape[0]
    heads = d_rows.shape[1]
    groups = input_map.shape[1]
    width_state = input_map.shape[2]
    ratio = heads // groups
    grad_f = d_rows.astype(jnp.float32)
    signal_f = signal.astype(jnp.float32)
    grad_skip = jnp.sum(grad_f * signal_f, axis=(0, 2))
    h_low = h_in.astype(jnp.bfloat16)
    carried_low = carried.astype(jnp.bfloat16)
    offset = jnp.exp(decay_sum)[:, :, None] * ein("thn,hpn->thp", output_heads, h_low)
    grad_sum = jnp.sum(grad_f * offset, axis=2)
    out_heads_grad = ein("thp,hpn->thn", scaled_grad, h_low)
    grad_weighted = ein("shn,hpn->shp", input_heads, carried_low)
    in_heads_grad = ein("shp,hpn->shn", weighted, carried_low)
    back = jnp.sum(grad_weighted * scaled.astype(jnp.float32), axis=2) * to_end
    end_term = jnp.exp(decay_sum[-1]) * jnp.sum(h_in * carried, axis=(1, 2))
    last_row = (lax.broadcasted_iota(jnp.int32, (length, 1), 0) == length - 1).astype(jnp.float32)
    grad_sum = grad_sum - back + last_row * (jnp.sum(back, axis=0) + end_term)[None, :]
    spread = decay_sum.T[:, :, None] - decay_sum.T[:, None, :]
    decay = jnp.where(lower[None] > 0, jnp.exp(jnp.minimum(spread, 0.0)), 0.0)
    score = ein("tgn,sgn->gts", output_map, input_map)
    mix = jnp.repeat(score, ratio, axis=0) * decay
    grad_mix = ein("thp,shp->hts", d_rows, scaled)
    grad_scaled = grad_weighted * to_end[:, :, None] + ein(
        "hts,thp->shp", mix.astype(jnp.bfloat16), d_rows
    )
    product = grad_mix * mix
    grad_sum = grad_sum + (jnp.sum(product, axis=2) - jnp.sum(product, axis=1)).T
    grad_score = jnp.sum((grad_mix * decay).reshape(groups, ratio, length, length), axis=1).astype(
        jnp.bfloat16
    )
    grad_outmap = ein("gts,sgn->tgn", grad_score, input_map) + jnp.sum(
        out_heads_grad.reshape(length, groups, ratio, width_state), axis=2
    )
    grad_in = ein("gts,tgn->sgn", grad_score, output_map) + jnp.sum(
        in_heads_grad.reshape(length, groups, ratio, width_state), axis=2
    )
    grad_log = jnp.dot(lower.T, grad_sum, precision=lax.Precision.HIGHEST)
    descent_increment = grad_log * rate + jnp.sum(grad_scaled * signal_f, axis=2)
    grad_signal = skip_gain[None, :, None] * grad_f + grad_scaled * step[:, :, None]
    grad_dt = descent_increment * jax.nn.sigmoid(dt_rows + dt_bias)
    decay_log_gradient = jnp.sum(grad_log * step, axis=0) * rate
    grad_act = jnp.concatenate(
        [
            grad_signal.reshape(length, heads * HDIM),
            grad_in.reshape(length, groups * width_state),
            grad_outmap.reshape(length, groups * width_state),
        ],
        axis=1,
    )
    return (grad_act, grad_dt, decay_log_gradient, jnp.sum(grad_dt, axis=0), grad_skip)


def link(earlier, later):
    return (earlier[0] + later[0], jnp.exp(later[0])[:, None, None] * earlier[1] + later[1])


def link_blocks(lower_pair, upper_pair):
    zero_rate = jnp.zeros_like(lower_pair[0])
    zero_state = jnp.zeros_like(lower_pair[1])
    below = prefix(lower_pair, "ctx", link, (zero_rate, zero_state), False)
    beyond = prefix(upper_pair, "ctx", link, (zero_rate, zero_state), True)
    total = jax.tree.map(
        lambda part: broadcast(part, "ctx", lax.axis_size("ctx") - 1), link(below, lower_pair)
    )
    return jnp.stack([below[1], link(total, beyond)[1]])


def conv_back(grad_pre, wide_grad, kernel_taps, padded, at_end, length):
    rim = kernel_taps.shape[0] - 1
    after = jnp.stack(
        [jnp.where(at_end, grad_pre[1, :rim], wide_grad[3 * rim : 4 * rim]), wide_grad[0:rim]]
    )
    padded_next = jnp.concatenate([grad_pre, after], axis=1)
    grad_raw = jnp.zeros(grad_pre.shape, jnp.float32)
    for tap in range(rim + 1):
        grad_raw = (
            grad_raw
            + kernel_taps[tap][None, None, :] * padded_next[:, rim - tap : rim - tap + length]
        )
    tap_grads = jnp.stack(
        [jnp.sum(grad_pre * padded[:, tap : tap + length], axis=(0, 1)) for tap in range(rim + 1)]
    )
    return (grad_raw, tap_grads, jnp.sum(grad_pre, axis=(0, 1)))


def first_rows(grad_pre, rim):
    return jnp.concatenate([grad_pre[0, :rim], grad_pre[1, :rim]], axis=0)


def shards(
    sig_raw,
    map_raw,
    step_size_logits,
    d_out,
    sig_taps,
    map_taps,
    sig_bias,
    map_bias,
    a_log,
    dt_bias,
    skip_gain,
):
    all_map_taps, all_map_bias = (
        lax.all_gather(map_taps, "fsdp", axis=1, tiled=True),
        lax.all_gather(map_bias, "fsdp", axis=0, tiled=True),
    )
    kernel_taps = jnp.concatenate([sig_taps, all_map_taps], axis=1)
    kernel_bias = jnp.concatenate([sig_bias, all_map_bias], axis=0)
    kernel = kernel_taps.shape[0]
    rim = kernel - 1
    length = sig_raw.shape[0] // 2
    sig_width = sig_raw.shape[1]
    map_width = map_raw.shape[1]
    width = sig_width + map_width
    heads_here = step_size_logits.shape[1]
    ratio = HEADS // GROUPS
    group_count = max(1, heads_here // ratio)
    first_group = lax.axis_index("fsdp") * heads_here // ratio
    fsdp_count = lax.axis_size("fsdp")
    owned = map_width // fsdp_count
    map_start = lax.axis_index("fsdp") * owned
    raw_rows = jnp.concatenate([sig_raw, map_raw], axis=1).reshape(2, length, width)
    tails = jnp.concatenate([raw_rows[1, length - rim :], raw_rows[0, length - rim :]], axis=0)
    wide = extended(tails, (("ctx", 0),), rim)
    at_end = lax.axis_index("ctx") == lax.axis_size("ctx") - 1
    before = jnp.stack(
        [wide[0:rim], jnp.where(at_end, raw_rows[0, length - rim :], wide[3 * rim : 4 * rim])]
    )
    padded = jnp.concatenate([before, raw_rows], axis=1).astype(jnp.float32)
    preact = kernel_bias[None, None, :] + jnp.zeros((2, length, width), jnp.float32)
    for tap in range(kernel):
        preact = preact + kernel_taps[tap][None, None, :] * padded[:, tap : tap + length]
    activated = jax.nn.silu(preact).astype(jnp.bfloat16)
    maps_all = activated[:, :, sig_width:].reshape(2, length, 2, GROUPS, STATE)
    maps_mine = lax.dynamic_slice_in_dim(maps_all, first_group, group_count, 3)
    local_act = jnp.concatenate(
        [activated[:, :, :sig_width], maps_mine.reshape(2, length, 2 * group_count * STATE)], axis=2
    )
    dt_rows = step_size_logits.reshape(2, length, heads_here)
    grad_rows = d_out.reshape(2, length, heads_here, HDIM)

    def parts_of(act_block, dt_block):
        return block_parts(act_block, dt_block, a_log, dt_bias, group_count)

    parts = jax.vmap(parts_of)(local_act, dt_rows)
    scaled_grad, state_grad = jax.vmap(entry_grad)(parts, grad_rows)
    ends = parts[8][:, -1]
    h_ins = link_blocks((ends[0], parts[12][0]), (ends[1], parts[12][1]))
    carried_pair = link_blocks((ends[1], state_grad[1]), (ends[0], state_grad[0]))
    carried = jnp.stack([carried_pair[1], carried_pair[0]])
    grad_act, grad_dt, decay_log_gradient, grad_dtb, grad_skip = jax.vmap(
        block_grads, in_axes=(0, 0, 0, 0, 0, None, 0, None)
    )(parts, grad_rows, scaled_grad, h_ins, carried, skip_gain, dt_rows, dt_bias)
    slope = silu_slope(preact)
    grad_pre_sig = grad_act[:, :, :sig_width] * slope[:, :, :sig_width]
    grad_mine = grad_act[:, :, sig_width:].reshape(2, length, 2, group_count, STATE)
    zero_index = jnp.zeros((), jnp.int32)
    placed = lax.dynamic_update_slice(
        jnp.zeros((2, length, 2, GROUPS, STATE), jnp.float32),
        grad_mine,
        (zero_index, zero_index, zero_index, first_group, zero_index),
    )
    map_term = placed.reshape(2, length, map_width)
    map_owned = lax.psum_scatter(map_term, "fsdp", scatter_dimension=2, tiled=True)
    map_slope = lax.dynamic_slice_in_dim(slope[:, :, sig_width:], map_start, owned, 2)
    grad_pre = jnp.concatenate([grad_pre_sig, map_owned * map_slope], axis=2)
    own_taps = jnp.concatenate([sig_taps, map_taps], axis=1)
    own_padded = jnp.concatenate(
        [
            padded[:, :, :sig_width],
            lax.dynamic_slice_in_dim(padded[:, :, sig_width:], map_start, owned, 2),
        ],
        axis=2,
    )
    wide_grad = extended(first_rows(grad_pre, rim), (("ctx", 0),), rim)
    grad_raw, tap_grads, bias_grads = conv_back(
        grad_pre, wide_grad, own_taps, own_padded, at_end, length
    )
    map_raw_grad = grad_raw[:, :, sig_width:]
    map_tap_grad = tap_grads[:, sig_width:]
    map_bias_grad = bias_grads[sig_width:]
    sig_raw_grad = grad_raw[:, :, :sig_width]
    sig_tap_grad = tap_grads[:, :sig_width]
    sig_bias_grad = bias_grads[:sig_width]
    reduced = lax.psum(
        (
            sig_tap_grad,
            map_tap_grad,
            sig_bias_grad,
            map_bias_grad,
            jnp.sum(decay_log_gradient, axis=0),
            jnp.sum(grad_dtb, axis=0),
            jnp.sum(grad_skip, axis=0),
        ),
        "ctx",
    )
    scale = 1.0 / math.sqrt(float(lax.axis_size("ctx") * 2 * length))
    final = jax.tree.map(lambda grad_part: grad_part * scale, reduced)
    return (
        sig_raw_grad.reshape(2 * length, sig_width),
        map_raw_grad.reshape(2 * length, owned),
        grad_dt.reshape(2 * length, heads_here),
        final[0],
        final[1],
        final[2],
        final[3],
        final[4],
        final[5],
        final[6],
    )


def solution(mesh):
    return jax.shard_map(
        shards,
        mesh=mesh,
        in_specs=(
            P("ctx", "fsdp"),
            P("ctx", None),
            P("ctx", "fsdp"),
            P("ctx", "fsdp"),
            P(None, "fsdp"),
            P(None, "fsdp"),
            P("fsdp"),
            P("fsdp"),
            P("fsdp"),
            P("fsdp"),
            P("fsdp"),
        ),
        out_specs=(
            P("ctx", "fsdp"),
            P("ctx", "fsdp"),
            P("ctx", "fsdp"),
            P(None, "fsdp"),
            P(None, "fsdp"),
            P("fsdp"),
            P("fsdp"),
            P("fsdp"),
            P("fsdp"),
            P("fsdp"),
        ),
        check_vma=False,
    )
```

profile of v0, /device:TPU:8, one launch (start us, length us, event | category | flops | bytes accessed | tf_op | source)
XLA Modules:
  0.0 1140.5 jit_solution(17790287372586400187)
XLA Ops:
  7.3 1.1 pad_maximum_fusion
  8.4 11.3 collective-permute-start.1
  19.7 1.9 collective-permute-start
  23.5 23.8 %all_gather.28 = f32[4,2048]{1,0:T(4,128)S(1)} all-gather(f32[4,128]{1,0:T(4,128)S(1)} %copy-done.35), channel_id=1, replica_groups=mesh['ctx'=32,'fsdp'=16] {'fsdp'}, dimensions={1}, use_global_device_ids=true | all-gather | bytes 34816 | tf_op jit(solution)/shard_map/all_gather | solution.py:222
  47.4 19.2 %all-gather.2 = f32[16,1,128]{2,1,0:T(1,128)S(1)} all-gather(f32[1,1,128]{2,1,0:T(1,128)S(1)} %bitcast.192), channel_id=1, replica_groups=mesh['ctx'=32,'fsdp'=16] {'fsdp'}, dimensions={0}, use_global_device_ids=true | all-gather | bytes 8704 | tf_op jit(solution)/shard_map/all_gather | solution.py:223
  66.8 2.0 add_multiply_fusion
  77.1 64.7 %all-gather.1 = f32[32,1,8]{2,1,0:T(1,128)} all-gather(f32[1,1,8]{2,1,0:T(1,128)S(1)} %copy.105), channel_id=3, replica_groups=mesh['ctx'=32,'fsdp'=16] {'ctx'}, dimensions={0}, use_global_device_ids=true | all-gather | bytes 1056 | tf_op jit(solution)/shard_map/all_gather | solution.py:17
  141.8 61.2 %all-gather = f32[32,1,8]{2,1,0:T(1,128)} all-gather(f32[1,1,8]{2,1,0:T(1,128)S(1)} %copy.101), channel_id=2, replica_groups=mesh['ctx'=32,'fsdp'=16] {'ctx'}, dimensions={0}, use_global_device_ids=true | all-gather | bytes 1056 | tf_op jit(solution)/shard_map/all_gather | solution.py:17
  204.2 1.1 fusion.21
  206.1 8.7 all-gather.12.cloned.1.call-done
  214.8 28.4 %while.54 = (s32[]{:T(128)}, f32[8,64,128]{2,1,0:T(8,128)S(1)}, s32[]{:T(128)}, f32[32,8]{1,0:T(8,128)}, f32[32,8,64,128]{3,2,1,0:T(8,128)}, /*index=5*/s32[]{:T(128)}, s32[]{:T(128)}, s32[]{:T(128)}) while((s32[]{:T(128)}, f32[8,64,128]{2,1,0:T(8,128)S(1)}, s32[]{:T(128)}, f32[32,8]{1,0:T(8,128)}, f32[32,8,64,128]{3,2,1,0:T(8,128)}, ...), condition=%wide.region_7.8_spmd, body=%wide.region_6.7_spmd.sunk | while | flops 131077 | bytes 786663 | solution.py:26
  244.1 115.7 %all-gather.10.cloned.1.call-done = f32[32,8,64,128]{3,2,1,0:T(8,128)} async-done(((f32[1,8,64,128]{3,2,1,0:T(8,128)}), f32[32,8,64,128]{3,2,1,0:T(8,128)}) %all-gather.10.cloned.1.call-update) | async-done | bytes 8388624 | tf_op jit(solution)/shard_map/all_gather | solution.py:17
  359.8 28.3 %while.53 = (s32[]{:T(128)}, f32[8,64,128]{2,1,0:T(8,128)S(1)}, s32[]{:T(128)}, f32[32,8]{1,0:T(8,128)}, f32[32,8,64,128]{3,2,1,0:T(8,128)}, /*index=5*/s32[]{:T(128)}, s32[]{:T(128)}, s32[]{:T(128)}) while((s32[]{:T(128)}, f32[8,64,128]{2,1,0:T(8,128)S(1)}, s32[]{:T(128)}, f32[32,8]{1,0:T(8,128)}, f32[32,8,64,128]{3,2,1,0:T(8,128)}, ...), condition=%wide.region_3.4_spmd, body=%wide.region_2.3_spmd.sunk | while | flops 131077 | bytes 786663 | solution.py:26
  388.9 115.5 %all-gather.14.cloned.1.call-done = f32[32,8,64,128]{3,2,1,0:T(8,128)} async-done(((f32[1,8,64,128]{3,2,1,0:T(8,128)}), f32[32,8,64,128]{3,2,1,0:T(8,128)}) %all-gather.14.cloned.1.call-update) | async-done | bytes 8388624 | tf_op jit(solution)/shard_map/all_gather | solution.py:17
  504.5 26.7 %while.55 = (s32[]{:T(128)}, f32[8]{0:T(128)S(1)}, f32[8,64,128]{2,1,0:T(8,128)S(1)}, s32[]{:T(128)}, f32[32,8]{1,0:T(8,128)}, /*index=5*/f32[32,8,64,128]{3,2,1...) while((s32[]{:T(128)}, f32[8]{0:T(128)S(1)}, f32[8,64,128]{2,1,0:T(8,128)S(1)}, s32[]{:T(128)}, ...), condition=%wide.region_9.10_spmd, body=%wide.region_8.9_spmd.sunk | while | flops 131086 | bytes 786755 | solution.py:26
  515.9 1.1 bitcast_add_fusion.17
  531.3 117.5 %all-gather.8.cloned.1.call-done = f32[32,8,64,128]{3,2,1,0:T(8,128)} async-done(((f32[1,8,64,128]{3,2,1,0:T(8,128)}), f32[32,8,64,128]{3,2,1,0:T(8,128)}) %all-gather.8.cloned.1.call-update) | async-done | bytes 8388624 | tf_op jit(solution)/shard_map/all_gather | solution.py:17
  648.8 26.7 %while.52 = (s32[]{:T(128)}, f32[8]{0:T(128)S(1)}, f32[8,64,128]{2,1,0:T(8,128)S(1)}, s32[]{:T(128)}, f32[32,8]{1,0:T(8,128)}, /*index=5*/f32[32,8,64,128]{3,2,1...) while((s32[]{:T(128)}, f32[8]{0:T(128)S(1)}, f32[8,64,128]{2,1,0:T(8,128)S(1)}, s32[]{:T(128)}, ...), condition=%wide.region_1.2_spmd, body=%wide.region_0.1_spmd.sunk | while | flops 131086 | bytes 786755 | solution.py:26
  675.5 226.0 %all-reduce.4.cloned.1.call-done = (f32[8,64,128]{2,1,0:T(8,128)}, f32[8,64,128]{2,1,0:T(8,128)}) async-done(((f32[8,64,128]{2,1,0:T(8,128)}, f32[8,64,128]{2,1,0:T(8,128)}), (f32[8,64,128]{2,1,0:T(8,128)}, f32[8,64,128]{2,1,0:T(8,128)})) %all-reduce.4.cloned.1.call-update) | async-done | bytes 524304 | tf_op jit(solution)/shard_map/psum | solution.py:31
  901.6 1.2 add_bitcast_fusion
  903.8 2.8 dynamic_update_slice.3
  906.5 1.1 reshape.195
  908.8 1.3 copy-done.1
  910.1 1.1 slice.218
  911.6 1.3 fusion.13
  912.9 2.3 multiply_reduce_fusion
  915.2 1.3 copy.112
  917.5 73.3 %reduce-scatter.2.cloned.1.call-done = f32[2,64,128]{2,1,0:T(8,128)} async-done(((f32[2,64,2048]{2,1,0:T(8,128)}), f32[2,64,128]{2,1,0:T(8,128)}) %reduce-scatter.2.cloned.1.call-update) | async-done | bytes 65552 | tf_op jit(solution)/shard_map/reduce_scatter | solution.py:282
  991.7 6.6 collective-permute-start.2
  999.6 1.9 collective-permute-start.3
  1002.3 5.3 collective-permute-done.3
  1009.5 120.4 %all-reduce = (f32[4,512]{1,0:T(4,128)S(1)}, f32[4,128]{1,0:T(4,128)S(1)}, f32[512]{0:T(512)S(1)}, f32[128]{0:T(128)S(1)}, f32[8]{0:T(128)S(1)}, /*index=5*/f32[8]{0:T(128)S(1)}, f32[8]{0:T(128)S(1)}) all-reduce(f32[4,512]{1,0:T(4,128)S(1)} %slice.240, ...), channel_id=1, replica_groups=mesh['ctx'=32,'fsdp'=16] {'ctx'}, use_global_device_ids=true, to_apply=%region_23.24 | all-reduce | flops 3224 | bytes 25792 | tf_op jit(solution)/shard_map/psum | solution.py:303
  (340 shorter events, 133.3 us)
Async XLA Ops:
  7.2 59.3 %copy-start.42 = (f32[512]{0:T(512)S(1)}, f32[512]{0:T(512)}, u32[]{:S(2)}) copy-start(f32[512]{0:T(512)} %param.25) | copy-start | bytes 6148
  7.3 207.5 %all-gather.12.cloned.1.call-start = ((), (), s32[]{:S(2)}) async-start(), calls=%async_computation.3 | async-start | bytes 8650752 | tf_op jit(solution)/shard_map/all_gather | solution.py:17
  8.4 58.1 %collective-permute-start.1 = (bf16[3,2560]{1,0:T(4,128)(2,1)S(1)}, bf16[3,2560]{1,0:T(4,128)(2,1)S(1)}, u32[]{:S(2)}, u32[]{:S(2)}) collective-permute-start(bf16[3,2560]{1,0:T(4,128)(2,1)S(1)} %get-tuple-element.414), channel_id=1, source_target_pairs={{16,0},{32,16},{48,32},{64,48},{80,64},{96,80},{112,96},{128,112},... | collective-permute-start | bytes 46088 | tf_op jit(solution)/shard_map/ppermute | solution.py:42
  19.7 46.8 %collective-permute-start = (bf16[3,2560]{1,0:T(4,128)(2,1)S(1)}, bf16[3,2560]{1,0:T(4,128)(2,1)S(1)}, u32[]{:S(2)}, u32[]{:S(2)}) collective-permute-start(bf16[3,2560]{1,0:T(4,128)(2,1)S(1)} %get-tuple-element.413), channel_id=1, source_target_pairs={{0,16},{16,32},{32,48},{48,64},{64,80},{80,96},{96,112},{112,128},... | collective-permute-start | bytes 46088 | tf_op jit(solution)/shard_map/ppermute | solution.py:39
  21.9 47.6 %copy-start.25 = (f32[2,64,8]{1,2,0:T(8,128)}, f32[2,64,8]{1,2,0:T(8,128)S(1)}, u32[]{:S(2)}) copy-start(f32[2,64,8]{1,2,0:T(8,128)S(1)} %compare_select_fusion) | copy-start | bytes 12292
  66.8 842.0 %copy-start = (f32[2,67,2560]{2,1,0:T(8,128)}, f32[2,67,2560]{2,1,0:T(8,128)S(1)}, u32[]{:S(2)}) copy-start(f32[2,67,2560]{2,1,0:T(8,128)S(1)} %maximum_convert_fusion) | copy-start | bytes 4116484
  69.9 833.3 %copy-start.2 = (bf16[2,64,8,64]{1,3,2,0:T(8,128)(2,1)}, bf16[2,64,8,64]{1,3,2,0:T(8,128)(2,1)S(1)}, u32[]{:S(2)}) copy-start(bf16[2,64,8,64]{1,3,2,0:T(8,128)(2,1)S(1)} %multiply_convert_fusion.1) | copy-start | bytes 393220
  72.2 287.6 %all-gather.10.cloned.1.call-start = ((), (), s32[]{:S(2)}) async-start(), calls=%async_computation.2 | async-start | bytes 8650752 | tf_op jit(solution)/shard_map/all_gather | solution.py:17
  72.7 131.5 %copy-start.6 = (bf16[2,64,8,64]{1,3,2,0:T(8,128)(2,1)}, bf16[2,64,8,64]{1,3,2,0:T(8,128)(2,1)S(1)}, u32[]{:S(2)}) copy-start(bf16[2,64,8,64]{1,3,2,0:T(8,128)(2,1)S(1)} %copy.99) | copy-start | bytes 393220
  72.7 130.2 %copy-start.36 = (f32[4,128]{1,0:T(4,128)S(1)}, f32[4,128]{1,0:T(4,128)}, u32[]{:S(2)}) copy-start(f32[4,128]{1,0:T(4,128)} %param.24) | copy-start | bytes 6148
  74.7 429.8 %all-gather.14.cloned.1.call-start = ((), (), s32[]{:S(2)}) async-start(), calls=%async_computation.4 | async-start | bytes 8650752 | tf_op jit(solution)/shard_map/all_gather | solution.py:17
  75.4 573.3 %all-gather.8.cloned.1.call-start = ((), (), s32[]{:S(2)}) async-start(), calls=%async_computation.1 | async-start | bytes 8650752 | tf_op jit(solution)/shard_map/all_gather | solution.py:17
  76.0 825.5 %all-reduce.4.cloned.1.call-start = ((), (), s32[]{:S(2)}) async-start(), calls=%async_computation.6 | async-start | bytes 1048576 | tf_op jit(solution)/shard_map/psum | solution.py:31
  77.1 137.7 %copy-start.37 = (pred[64,64]{0,1:T(8,128)(4,1)}, pred[64,64]{0,1:T(8,128)(4,1)S(1)}, u32[]{:S(2)}) copy-start(pred[64,64]{0,1:T(8,128)(4,1)S(1)} %copy.109) | copy-start | bytes 12292
  531.2 459.5 %reduce-scatter.2.cloned.1.call-start = ((), (), s32[]{:S(2)}) async-start(), calls=%async_computation.5 | async-start | bytes 1114112 | tf_op jit(solution)/shard_map/reduce_scatter | solution.py:282
  675.4 227.3 %copy-start.7 = (bf16[2,64,8,64]{1,3,2,0:T(8,128)(2,1)S(1)}, bf16[2,64,8,64]{1,3,2,0:T(8,128)(2,1)}, u32[]{:S(2)}) copy-start(bf16[2,64,8,64]{1,3,2,0:T(8,128)(2,1)} %copy-done.6) | copy-start | bytes 393220
  675.5 227.3 %copy-start.20 = (f32[2,64,8]{1,2,0:T(8,128)S(1)}, f32[2,64,8]{1,2,0:T(8,128)}, u32[]{:S(2)}) copy-start(f32[2,64,8]{1,2,0:T(8,128)} %get-tuple-element.430) | copy-start | bytes 12292
  675.5 227.6 %copy-start.19 = (bf16[2,64,64]{1,2,0:T(8,128)(2,1)S(1)}, bf16[2,64,64]{1,2,0:T(8,128)(2,1)}, u32[]{:S(2)}) copy-start(bf16[2,64,64]{1,2,0:T(8,128)(2,1)} %copy-done.18) | copy-start | bytes 49156
  916.8 81.5 %copy-start.27 = (f32[64,64]{1,0:T(8,128)S(1)}, f32[64,64]{1,0:T(8,128)}, u32[]{:S(2)}) copy-start(f32[64,64]{1,0:T(8,128)} %fusion.61) | copy-start | bytes 49156
  916.8 81.5 %copy-start.29 = (f32[2,64,8]{1,0,2:T(2,128)S(1)}, f32[2,64,8]{1,0,2:T(2,128)}, u32[]{:S(2)}) copy-start(f32[2,64,8]{1,0,2:T(2,128)} %copy-done.28) | copy-start | bytes 12292
  916.8 81.5 %copy-start.45 = (f32[8]{0:T(128)S(1)}, f32[8]{0:T(128)}, u32[]{:S(2)}) copy-start(f32[8]{0:T(128)} %param.28) | copy-start | bytes 100
  916.8 81.5 %copy-start.47 = (f32[8]{0:T(128)S(1)}, f32[8]{0:T(128)}, u32[]{:S(2)}) copy-start(f32[8]{0:T(128)} %copy-done.46) | copy-start | bytes 100
  916.8 81.5 %copy-start.50 = (f32[64]{0:T(128)S(1)}, f32[64]{0:T(128)}, u32[]{:S(2)}) copy-start(f32[64]{0:T(128)} %compare_convert_fusion) | copy-start | bytes 772
  916.8 81.5 %copy-start.51 = (f32[2,8,64]{2,1,0:T(8,128)S(1)}, f32[2,8,64]{2,1,0:T(8,128)}, u32[]{:S(2)}) copy-start(f32[2,8,64]{2,1,0:T(8,128)} %get-tuple-element.336) | copy-start | bytes 12292
  916.8 81.5 %copy-start.52 = (f32[2,8,64]{2,1,0:T(8,128)S(1)}, f32[2,8,64]{2,1,0:T(8,128)}, u32[]{:S(2)}) copy-start(f32[2,8,64]{2,1,0:T(8,128)} %get-tuple-element.337) | copy-start | bytes 12292
  917.4 90.2 %slice-start = ((f32[2,67,2560]{2,1,0:T(8,128)}), f32[2,67,512]{2,1,0:T(8,128)S(1)}, s32[]{:S(2)}) async-start(f32[2,67,2560]{2,1,0:T(8,128)} %copy-done), calls=%async_computation.7 | async-start | bytes 589824 | tf_op jit(solution)/shard_map/slice | solution.py:288
  917.4 90.2 %copy-start.30 = (f32[640]{0:T(1024)S(1)}, f32[640]{0:T(1024)}, u32[]{:S(2)}) copy-start(f32[640]{0:T(1024)} %get-tuple-element.344) | copy-start | bytes 7684
  917.4 90.2 %copy-start.31 = (f32[640]{0:T(1024)S(1)}, f32[640]{0:T(1024)}, u32[]{:S(2)}) copy-start(f32[640]{0:T(1024)} %get-tuple-element.345) | copy-start | bytes 7684
  917.4 90.2 %copy-start.32 = (f32[640]{0:T(1024)S(1)}, f32[640]{0:T(1024)}, u32[]{:S(2)}) copy-start(f32[640]{0:T(1024)} %get-tuple-element.346) | copy-start | bytes 7684
  917.5 90.2 %copy-start.33 = (f32[640]{0:T(1024)S(1)}, f32[640]{0:T(1024)}, u32[]{:S(2)}) copy-start(f32[640]{0:T(1024)} %get-tuple-element.347) | copy-start | bytes 7684
  991.7 8.0 collective-permute-start.2
  999.6 7.9 collective-permute-start.3
  (33 other events, 277.5 us)
Sparse Core Ops, SparseCore 0:
  72.4 142.3 all-gather.11
  216.9 142.8 all-gather.9
  361.9 142.5 all-gather.13
  506.4 142.3 all-gather.7
  651.5 249.9 all-reduce.3
  907.8 82.9 reduce-scatter.1
where the time goes:
time: 1140 us
  waiting for transfers between devices  664 us (58%)
  blocking collectives  289 us (25%)
  other arithmetic  101 us (9%)
  local copies, waits for them, and re-layouts  39.5 us (3%)
  starting transfers between devices  22 us (2%)
  between operations  15.1 us (1%)
    all_gather x4, waiting for transfers between devices, prefix(): gathered = jax.tree.map(lambda a: lax.all_gather(a, axis), part)  357 us
    psum x1, waiting for transfers between devices, broadcast(): return lax.psum(jnp.where(mine, x, jnp.zeros_like(x)), axis)  226 us
    all_gather x2, blocking collectives, prefix(): gathered = jax.tree.map(lambda a: lax.all_gather(a, axis), part)  126 us
    psum x1, blocking collectives, shards(): lax.psum((sig_tap_grad, map_tap_grad, sig_bias_grad, map_bias_grad, jnp.s...  120 us
    reduce_scatter x1, waiting for transfers between devices, shards(): lax.psum_scatter(map_term, 'fsdp', scatter_dimension=2, tiled=True)  73.3 us
    add x62, other arithmetic, link(): jnp.exp(later[0])[:, None, None] * earlier[1] + later[1]  65.5 us
    all_gather x1, blocking collectives, shards(): lax.all_gather(map_taps, 'fsdp', axis=1, tiled=True)  23.8 us
  transfers between devices with their start and end apart: 10, of which 8 were waited for; matrix products, arithmetic and copies ran while one was open for 11% of the time, Pallas kernels for 0%

commit v1 on v0

--- a/solution.py
+++ b/solution.py
@@ -28,7 +28,7 @@
 
 def broadcast(x, axis, root):
     mine = lax.axis_index(axis) == root
-    return lax.psum(jnp.where(mine, x, jnp.zeros_like(x)), axis)
+    return jnp.sum(lax.all_gather(jnp.where(mine, x, jnp.zeros_like(x)), axis), axis=0)
 
 
 def extended(block, sides, width):

time: 1140 us -> 1190 us (1.044)
  waiting for transfers between devices: 664 us -> 722 us
    all_gather x0 -> x2, waiting for transfers between devices: none -> 246 us  [broadcast(): lax.all_gather(jnp.where(mine, x, jnp.zeros_like(x)), axis)]
    psum x1 -> x0, waiting for transfers between devices: 226 us -> none  [broadcast(): return lax.psum(jnp.where(mine, x, jnp.zeros_like(x)), axis)]
    all_gather x4, waiting for transfers between devices: 357 us -> 394 us  [prefix(): gathered = jax.tree.map(lambda a: lax.all_gather(a, axis), part)]
  transfers between devices with their start and end apart: 10 -> 11, of which waited for: 8 -> 9; matrix products, arithmetic and copies ran while one was open for 11% -> 9% of each run, Pallas kernels for 0% -> 0%
where the time goes in v1:
time: 1190 us; the launch traced here: 1180 us
  waiting for transfers between devices  722 us (61%)
  blocking collectives  290 us (24%)
  other arithmetic  97.6 us (8%)
  local copies, waits for them, and re-layouts  28.9 us (2%)
  starting transfers between devices  22 us (2%)
  between operations  15.2 us (1%)
    all_gather x4, waiting for transfers between devices, prefix(): gathered = jax.tree.map(lambda a: lax.all_gather(a, axis), part)  394 us
    all_gather x2, waiting for transfers between devices, broadcast(): lax.all_gather(jnp.where(mine, x, jnp.zeros_like(x)), axis)  246 us
    all_gather x2, blocking collectives, prefix(): gathered = jax.tree.map(lambda a: lax.all_gather(a, axis), part)  127 us
    psum x1, blocking collectives, shards(): lax.psum((sig_tap_grad, map_tap_grad, sig_bias_grad, map_bias_grad, jnp.s...  120 us
    reduce_scatter x1, waiting for transfers between devices, shards(): lax.psum_scatter(map_term, 'fsdp', scatter_dimension=2, tiled=True)  73.8 us
    add x62, other arithmetic, link(): jnp.exp(later[0])[:, None, None] * earlier[1] + later[1]  65.7 us
  transfers between devices with their start and end apart: 11, of which 9 were waited for; matrix products, arithmetic and copies ran while one was open for 9% of the time, Pallas kernels for 0%

profile of v1, /device:TPU:8, one launch (start us, length us, event | category | flops | bytes accessed | tf_op | source)
XLA Modules:
  0.0 1184.7 jit_solution(1666781651121969397)
XLA Ops:
  7.3 1.1 pad_maximum_fusion
  8.5 11.3 collective-permute-start.1
  19.8 1.9 collective-permute-start
  22.3 23.8 %all_gather.40 = f32[4,2048]{1,0:T(4,128)S(1)} all-gather(f32[4,128]{1,0:T(4,128)S(1)} %copy-done.34), channel_id=1, replica_groups=mesh['ctx'=32,'fsdp'=16] {'fsdp'}, dimensions={1}, use_global_device_ids=true | all-gather | bytes 34816 | tf_op jit(solution)/shard_map/all_gather | solution.py:222
  46.2 19.2 %all-gather.4 = f32[16,1,128]{2,1,0:T(1,128)S(1)} all-gather(f32[1,1,128]{2,1,0:T(1,128)S(1)} %bitcast.199), channel_id=1, replica_groups=mesh['ctx'=32,'fsdp'=16] {'fsdp'}, dimensions={0}, use_global_device_ids=true | all-gather | bytes 8704 | tf_op jit(solution)/shard_map/all_gather | solution.py:223
  66.8 2.0 add_multiply_fusion
  72.6 62.7 %all-gather.1 = f32[32,1,8]{2,1,0:T(1,128)S(1)} all-gather(f32[1,1,8]{2,1,0:T(1,128)S(1)} %copy.105), channel_id=3, replica_groups=mesh['ctx'=32,'fsdp'=16] {'ctx'}, dimensions={0}, use_global_device_ids=true | all-gather | bytes 1056 | tf_op jit(solution)/shard_map/all_gather | solution.py:17
  135.3 78.9 %all-gather.14.cloned.1.call-done = f32[32,8,64,128]{3,2,1,0:T(8,128)} async-done(((f32[1,8,64,128]{3,2,1,0:T(8,128)}), f32[32,8,64,128]{3,2,1,0:T(8,128)}) %all-gather.14.cloned.1.call-update) | async-done | bytes 8388624 | tf_op jit(solution)/shard_map/all_gather | solution.py:17
  214.2 17.7 %while.53 = (s32[]{:T(128)}, f32[8,64,128]{2,1,0:T(8,128)S(1)}, s32[]{:T(128)}, f32[32,8]{1,0:T(8,128)S(1)}, f32[32,8,64,128]{3,2,1,0:T(8,128)}, /*index=5*/s32[]{:T(128)}, s32[]{:T(128)}, s32[]{:T(128)}) while((s32[]{:T(128)}, f32[8,64,128]{2,1,0:T(8,128)S(1)}, s32[]{:T(128)}, f32[32,8]{1,0:T(8,128)S(1)}, f32[32,8,64,128]{3,2,1,0:T(8,128)}, ...), condition=%wide.region_3.4_spmd, body=%wide.region_2.3_spmd.sunk | while | flops 131077 | bytes 786655 | solution.py:26
  232.9 63.9 %all-gather = f32[32,1,8]{2,1,0:T(1,128)S(1)} all-gather(f32[1,1,8]{2,1,0:T(1,128)S(1)} %copy.101), channel_id=2, replica_groups=mesh['ctx'=32,'fsdp'=16] {'ctx'}, dimensions={0}, use_global_device_ids=true | all-gather | bytes 1056 | tf_op jit(solution)/shard_map/all_gather | solution.py:17
  297.7 60.5 %all-gather.12.cloned.1.call-done = f32[32,8,64,128]{3,2,1,0:T(8,128)} async-done(((f32[1,8,64,128]{3,2,1,0:T(8,128)}), f32[32,8,64,128]{3,2,1,0:T(8,128)}) %all-gather.12.cloned.1.call-update) | async-done | bytes 8388624 | tf_op jit(solution)/shard_map/all_gather | solution.py:17
  358.2 16.7 %while.52 = (s32[]{:T(128)}, f32[8]{0:T(128)S(1)}, f32[8,64,128]{2,1,0:T(8,128)S(1)}, s32[]{:T(128)}, f32[32,8]{1,0:T(8,128)S(1)}, /*index=5*/f32[32,8,64,128]{3...) while((s32[]{:T(128)}, f32[8]{0:T(128)S(1)}, f32[8,64,128]{2,1,0:T(8,128)S(1)}, s32[]{:T(128)}, ...), condition=%wide.region_1.2_spmd, body=%wide.region_0.1_spmd.sunk | while | flops 131086 | bytes 786747 | solution.py:26
  375.5 127.9 %all-gather.20.cloned.1.call-done = f32[256,64,128]{2,1,0:T(8,128)} async-done(((f32[8,64,128]{2,1,0:T(8,128)}), f32[256,64,128]{2,1,0:T(8,128)}) %all-gather.20.cloned.1.call-update) | async-done | bytes 8388624 | tf_op jit(solution)/shard_map/all_gather | solution.py:31
  503.4 4.0 reduce_sum.202
  508.2 1.1 fusion.13
  511.7 142.1 %all-gather.16.cloned.1.call-done = f32[32,8,64,128]{3,2,1,0:T(8,128)} async-done(((f32[1,8,64,128]{3,2,1,0:T(8,128)}), f32[32,8,64,128]{3,2,1,0:T(8,128)}) %all-gather.16.cloned.1.call-update) | async-done | bytes 8388624 | tf_op jit(solution)/shard_map/all_gather | solution.py:17
  653.8 28.6 %while.54 = (s32[]{:T(128)}, f32[8,64,128]{2,1,0:T(8,128)S(1)}, s32[]{:T(128)}, f32[32,8]{1,0:T(8,128)}, f32[32,8,64,128]{3,2,1,0:T(8,128)}, /*index=5*/s32[]{:T(128)}, s32[]{:T(128)}, s32[]{:T(128)}) while((s32[]{:T(128)}, f32[8,64,128]{2,1,0:T(8,128)S(1)}, s32[]{:T(128)}, f32[32,8]{1,0:T(8,128)}, f32[32,8,64,128]{3,2,1,0:T(8,128)}, ...), condition=%wide.region_7.8_spmd, body=%wide.region_6.7_spmd.sunk | while | flops 131077 | bytes 786655 | solution.py:26
  683.6 1.1 fusion.21
  685.7 112.6 %all-gather.18.cloned.1.call-done = f32[32,8,64,128]{3,2,1,0:T(8,128)} async-done(((f32[1,8,64,128]{3,2,1,0:T(8,128)}), f32[32,8,64,128]{3,2,1,0:T(8,128)}) %all-gather.18.cloned.1.call-update) | async-done | bytes 8388624 | tf_op jit(solution)/shard_map/all_gather | solution.py:17
  798.3 26.7 %while.55 = (s32[]{:T(128)}, f32[8]{0:T(128)S(1)}, f32[8,64,128]{2,1,0:T(8,128)S(1)}, s32[]{:T(128)}, f32[32,8]{1,0:T(8,128)}, /*index=5*/f32[32,8,64,128]{3,2,1...) while((s32[]{:T(128)}, f32[8]{0:T(128)S(1)}, f32[8,64,128]{2,1,0:T(8,128)S(1)}, s32[]{:T(128)}, ...), condition=%wide.region_9.10_spmd, body=%wide.region_8.9_spmd.sunk | while | flops 131086 | bytes 786747 | solution.py:26
  825.0 118.3 %all-gather.22.cloned.1.call-done = f32[256,64,128]{2,1,0:T(8,128)} async-done(((f32[8,64,128]{2,1,0:T(8,128)}), f32[256,64,128]{2,1,0:T(8,128)}) %all-gather.22.cloned.1.call-update) | async-done | bytes 8388624 | tf_op jit(solution)/shard_map/all_gather | solution.py:31
  943.4 4.0 reduce_sum.205
  948.5 2.8 dynamic_update_slice.3
  951.3 1.1 reshape.195
  954.2 1.3 copy-done.1
  957.0 2.5 multiply_reduce_fusion
  959.4 1.2 copy.112
  961.7 73.8 %reduce-scatter.2.cloned.1.call-done = f32[2,64,128]{2,1,0:T(8,128)} async-done(((f32[2,64,2048]{2,1,0:T(8,128)}), f32[2,64,128]{2,1,0:T(8,128)}) %reduce-scatter.2.cloned.1.call-update) | async-done | bytes 65552 | tf_op jit(solution)/shard_map/reduce_scatter | solution.py:282
  1036.4 6.6 collective-permute-start.2
  1044.4 1.9 collective-permute-start.3
  1047.0 5.3 collective-permute-done.3
  1054.2 120.4 %all-reduce = (f32[4,512]{1,0:T(4,128)S(1)}, f32[4,128]{1,0:T(4,128)S(1)}, f32[512]{0:T(512)S(1)}, f32[128]{0:T(128)S(1)}, f32[8]{0:T(128)S(1)}, /*index=5*/f32[8]{0:T(128)S(1)}, f32[8]{0:T(128)S(1)}) all-reduce(f32[4,512]{1,0:T(4,128)S(1)} %slice.240, ...), channel_id=1, replica_groups=mesh['ctx'=32,'fsdp'=16] {'ctx'}, use_global_device_ids=true, to_apply=%region_23.24 | all-reduce | flops 3224 | bytes 25792 | tf_op jit(solution)/shard_map/psum | solution.py:303
  (343 shorter events, 114.3 us)
Async XLA Ops:
  7.3 206.9 %all-gather.14.cloned.1.call-start = ((), (), s32[]{:S(2)}) async-start(), calls=%async_computation.2 | async-start | bytes 8650752 | tf_op jit(solution)/shard_map/all_gather | solution.py:17
  8.5 58.0 %collective-permute-start.1 = (bf16[3,2560]{1,0:T(4,128)(2,1)S(1)}, bf16[3,2560]{1,0:T(4,128)(2,1)S(1)}, u32[]{:S(2)}, u32[]{:S(2)}) collective-permute-start(bf16[3,2560]{1,0:T(4,128)(2,1)S(1)} %get-tuple-element.416), channel_id=1, source_target_pairs={{16,0},{32,16},{48,32},{64,48},{80,64},{96,80},{112,96},{128,112},... | collective-permute-start | bytes 46088 | tf_op jit(solution)/shard_map/ppermute | solution.py:42
  19.8 46.7 %collective-permute-start = (bf16[3,2560]{1,0:T(4,128)(2,1)S(1)}, bf16[3,2560]{1,0:T(4,128)(2,1)S(1)}, u32[]{:S(2)}, u32[]{:S(2)}) collective-permute-start(bf16[3,2560]{1,0:T(4,128)(2,1)S(1)} %get-tuple-element.415), channel_id=1, source_target_pairs={{0,16},{16,32},{32,48},{48,64},{64,80},{80,96},{96,112},{112,128},... | collective-permute-start | bytes 46088 | tf_op jit(solution)/shard_map/ppermute | solution.py:39
  65.6 442.6 %copy-start.20 = (f32[2,64,8]{1,2,0:T(8,128)}, f32[2,64,8]{1,2,0:T(8,128)S(1)}, u32[]{:S(2)}) copy-start(f32[2,64,8]{1,2,0:T(8,128)S(1)} %compare_select_fusion) | copy-start | bytes 12292
  66.5 881.0 %copy-start.4 = (bf16[2,64,8,64]{1,3,2,0:T(8,128)(2,1)}, bf16[2,64,8,64]{1,3,2,0:T(8,128)(2,1)S(1)}, u32[]{:S(2)}) copy-start(bf16[2,64,8,64]{1,3,2,0:T(8,128)(2,1)S(1)} %copy.99) | copy-start | bytes 393220
  66.8 887.4 %copy-start = (f32[2,67,2560]{2,1,0:T(8,128)}, f32[2,67,2560]{2,1,0:T(8,128)S(1)}, u32[]{:S(2)}) copy-start(f32[2,67,2560]{2,1,0:T(8,128)S(1)} %maximum_convert_fusion) | copy-start | bytes 4116484
  69.9 144.3 %copy-start.13 = (bf16[2,64,128]{2,1,0:T(8,128)(2,1)}, bf16[2,64,128]{2,1,0:T(8,128)(2,1)S(1)}, u32[]{:S(2)}) copy-start(bf16[2,64,128]{2,1,0:T(8,128)(2,1)S(1)} %get-tuple-element.424) | copy-start | bytes 98308
  71.0 287.2 %all-gather.12.cloned.1.call-start = ((), (), s32[]{:S(2)}) async-start(), calls=%async_computation.1 | async-start | bytes 8650752 | tf_op jit(solution)/shard_map/all_gather | solution.py:17
  71.7 431.7 %all-gather.20.cloned.1.call-start = ((), (), s32[]{:S(2)}) async-start(), calls=%async_computation.6 | async-start | bytes 8650752 | tf_op jit(solution)/shard_map/all_gather | solution.py:31
  231.9 126.3 %copy-start.27 = (f32[32,8]{1,0:T(8,128)}, f32[32,8]{1,0:T(8,128)S(1)}, u32[]{:S(2)}) copy-start(f32[32,8]{1,0:T(8,128)S(1)} %get-tuple-element.720) | copy-start | bytes 3076
  232.8 421.0 %all-gather.16.cloned.1.call-start = ((), (), s32[]{:S(2)}) async-start(), calls=%async_computation.3 | async-start | bytes 8650752 | tf_op jit(solution)/shard_map/all_gather | solution.py:17
  297.7 210.4 %copy-start.10 = (f32[2,64,512]{1,2,0:T(8,128)}, f32[2,64,512]{1,2,0:T(8,128)S(1)}, u32[]{:S(2)}) copy-start(f32[2,64,512]{1,2,0:T(8,128)S(1)} %copy.113) | copy-start | bytes 786436
  374.9 128.5 %copy-start.28 = (f32[32,8]{1,0:T(8,128)}, f32[32,8]{1,0:T(8,128)S(1)}, u32[]{:S(2)}) copy-start(f32[32,8]{1,0:T(8,128)S(1)} %get-tuple-element.721) | copy-start | bytes 3076
  508.2 176.7 %copy-start.2 = (f32[1,8,64,128]{3,2,1,0:T(8,128)}, f32[1,8,64,128]{3,2,1,0:T(8,128)S(1)}, u32[]{:S(2)}) copy-start(f32[1,8,64,128]{3,2,1,0:T(8,128)S(1)} %add_bitcast_fusion.1) | copy-start | bytes 786436
  511.1 287.2 %all-gather.18.cloned.1.call-start = ((), (), s32[]{:S(2)}) async-start(), calls=%async_computation.4 | async-start | bytes 8650752 | tf_op jit(solution)/shard_map/all_gather | solution.py:17
  511.7 431.7 %all-gather.22.cloned.1.call-start = ((), (), s32[]{:S(2)}) async-start(), calls=%async_computation.7 | async-start | bytes 8650752 | tf_op jit(solution)/shard_map/all_gather | solution.py:31
  683.3 352.2 %reduce-scatter.2.cloned.1.call-start = ((), (), s32[]{:S(2)}) async-start(), calls=%async_computation.5 | async-start | bytes 1114112 | tf_op jit(solution)/shard_map/reduce_scatter | solution.py:282
  960.8 82.2 %copy-start.23 = (f32[2,64,8]{1,2,0:T(8,128)S(1)}, f32[2,64,8]{1,2,0:T(8,128)}, u32[]{:S(2)}) copy-start(f32[2,64,8]{1,2,0:T(8,128)} %copy-done.22) | copy-start | bytes 12292
  960.8 82.2 %copy-start.24 = (f32[64,64]{1,0:T(8,128)S(1)}, f32[64,64]{1,0:T(8,128)}, u32[]{:S(2)}) copy-start(f32[64,64]{1,0:T(8,128)} %fusion.61) | copy-start | bytes 49156
  960.8 82.2 %copy-start.26 = (f32[2,64,8]{1,0,2:T(2,128)S(1)}, f32[2,64,8]{1,0,2:T(2,128)}, u32[]{:S(2)}) copy-start(f32[2,64,8]{1,0,2:T(2,128)} %copy-done.25) | copy-start | bytes 12292
  960.9 82.2 %copy-start.45 = (f32[8]{0:T(128)S(1)}, f32[8]{0:T(128)}, u32[]{:S(2)}) copy-start(f32[8]{0:T(128)} %param.28) | copy-start | bytes 100
  960.9 82.2 %copy-start.47 = (f32[8]{0:T(128)S(1)}, f32[8]{0:T(128)}, u32[]{:S(2)}) copy-start(f32[8]{0:T(128)} %copy-done.46) | copy-start | bytes 100
  960.9 82.2 %copy-start.50 = (f32[64]{0:T(128)S(1)}, f32[64]{0:T(128)}, u32[]{:S(2)}) copy-start(f32[64]{0:T(128)} %compare_convert_fusion) | copy-start | bytes 772
  960.9 82.2 %copy-start.51 = (f32[2,8,64]{2,1,0:T(8,128)S(1)}, f32[2,8,64]{2,1,0:T(8,128)}, u32[]{:S(2)}) copy-start(f32[2,8,64]{2,1,0:T(8,128)} %get-tuple-element.336) | copy-start | bytes 12292
  960.9 82.2 %copy-start.52 = (f32[2,8,64]{2,1,0:T(8,128)S(1)}, f32[2,8,64]{2,1,0:T(8,128)}, u32[]{:S(2)}) copy-start(f32[2,8,64]{2,1,0:T(8,128)} %get-tuple-element.337) | copy-start | bytes 12292
  961.3 91.0 %slice-start.1 = ((f32[2,67,2560]{2,1,0:T(8,128)}), f32[2,67,512]{2,1,0:T(8,128)S(1)}, s32[]{:S(2)}) async-start(f32[2,67,2560]{2,1,0:T(8,128)} %copy-done), calls=%async_computation.9 | async-start | bytes 589824 | tf_op jit(solution)/shard_map/slice | solution.py:288
  961.3 91.0 %copy-start.29 = (f32[640]{0:T(1024)S(1)}, f32[640]{0:T(1024)}, u32[]{:S(2)}) copy-start(f32[640]{0:T(1024)} %get-tuple-element.344) | copy-start | bytes 7684
  961.3 91.0 %copy-start.30 = (f32[640]{0:T(1024)S(1)}, f32[640]{0:T(1024)}, u32[]{:S(2)}) copy-start(f32[640]{0:T(1024)} %get-tuple-element.345) | copy-start | bytes 7684
  961.4 91.0 %copy-start.31 = (f32[640]{0:T(1024)S(1)}, f32[640]{0:T(1024)}, u32[]{:S(2)}) copy-start(f32[640]{0:T(1024)} %get-tuple-element.346) | copy-start | bytes 7684
  961.4 91.0 %copy-start.32 = (f32[640]{0:T(1024)S(1)}, f32[640]{0:T(1024)}, u32[]{:S(2)}) copy-start(f32[640]{0:T(1024)} %get-tuple-element.347) | copy-start | bytes 7684
  1036.4 7.9 collective-permute-start.2
  1044.4 7.9 collective-permute-start.3
  (34 other events, 500.0 us)
Sparse Core Ops, SparseCore 0:
  71.1 143.0 all-gather.13
  216.8 141.3 all-gather.11
  360.3 143.0 all-gather.19
  511.2 142.5 all-gather.15
  655.7 142.5 all-gather.17
  800.8 142.5 all-gather.21
  952.5 82.9 reduce-scatter.1
